TPU v7x, 256 devices: a whole 4x4x8 slice. The times are simulated.
256 devices in a mesh: row: 8 (over y, x_hi), col: 32 (over x_lo, z, core).
Axes of the slice: x: 4 (x_hi: 2, x_lo: 2; x = x_hi * 2 + x_lo), y: 4, z: 8, core: 2. Of those that a mesh axis runs over, the one named last changes fastest.
Arguments:
- inverse_block: float32 [12288, 12288], P('row', 'col'), may hold values from -6 to 6
- factor_panel: float32 [3, 12288, 256], P(None, ('row', 'col')), may hold values from -0.0546875 to 0.0546875
- diag_inverse: float32 [3, 256, 256], P(None, 'row'), may hold values from -6 to 6
- block_lists: int32 [3, 48], replicated, may hold values from 0 to 47, as said below
- list_counts: int32 [3], replicated, may hold values from 6 to 48, as said below
Outputs:
- solved: float32 [3, 12288, 256], P(None, ('row', 'col'))
- diag_block: float32 [3, 256, 256], P(None, 'row')
Inputs may be any that keep to these rules, and one draw needn't show every extreme that they name: `block_lists`: row k is an ordering of all 48 ancestor blocks; its first list_counts[k] entries are the blocks listed for supernode k. `list_counts`: one supernode lists all 48 blocks and one lists 48 // 8 of them.
All inputs are finite; a program needn't handle non-finite values.
Results may differ from a plain program's by a relative error of at most 0.000071.
Values sent between devices are 32-bit elements; how exact they have to be, the bound alone decides.
No kernel may reach another device: no remote copies, remote signals or barrier semaphores. Data moves between devices by JAX's collectives and lax.ppermute only.
A program may use at most 64 MiB of HBM per device.

v0:
```python
import jax
import jax.numpy as jnp
from jax import lax
from jax.sharding import PartitionSpec as P

NA = 12288
BLK = 256
NSN = 3


def broadcast(block, axis, source):
    block = jnp.where(lax.axis_index(axis) == source, block, jnp.zeros_like(block))
    return lax.psum(block, axis)


def listed_table(block_lists, list_counts, nblocks):
    entries = jnp.arange(block_lists.shape[1], dtype=jnp.int32)
    active = entries[None, :] < list_counts[:, None]
    hits = (
        block_lists[:, :, None] == jnp.arange(nblocks, dtype=jnp.int32)[None, None, :]
    ) & active[:, :, None]
    return jnp.any(hits, axis=1).astype(jnp.float32)


def rows_mask(table, first_row, count):
    global_rows = first_row + jnp.arange(count, dtype=jnp.int32)
    onehot = (
        (global_rows // BLK)[:, None] == jnp.arange(table.shape[1], dtype=jnp.int32)[None, :]
    ).astype(jnp.float32)
    return jnp.dot(table, onehot.T, precision=lax.Precision.HIGHEST)


def apply_block(inverse_block, panels):
    panel_rows = panels[0]
    summed = jnp.dot(inverse_block, panel_rows, precision=lax.Precision.HIGHEST)
    results = [summed]
    return jnp.stack(results)


def per_device(inverse_block, factor_panel, diag_inverse, block_lists, list_counts):
    n_row = lax.axis_size("row")
    n_col = lax.axis_size("col")
    row_id = lax.axis_index("row")
    col_id = lax.axis_index("col")
    local_rows = factor_panel.shape[1]
    span_row = inverse_block.shape[0]
    span_col = inverse_block.shape[1]
    table = listed_table(block_lists, list_counts, NA // BLK)
    mask_local = rows_mask(table, (row_id * n_col + col_id) * local_rows, local_rows)
    mask_range = rows_mask(table, row_id * span_row, span_row)
    group_ratio = n_col // n_row
    source_row = col_id // group_ratio
    start_col = col_id % group_ratio * span_col
    solved_parts = []
    for member in range(NSN):
        gathered = lax.all_gather(factor_panel[member : member + 1], "col", axis=1, tiled=True)
        masked_range = gathered * mask_range[member : member + 1, :, None]
        piece = lax.dynamic_slice_in_dim(masked_range, start_col, span_col, 1)
        columns = broadcast(piece, "row", source_row)
        partial_value = (
            apply_block(inverse_block, columns) * mask_range[member : member + 1, :, None]
        )
        solved_parts.append(
            -lax.psum_scatter(partial_value, "col", scatter_dimension=1, tiled=True)
        )
    solved = jnp.concatenate(solved_parts, axis=0)
    masked_local = factor_panel * mask_local[:, :, None]
    terms = jnp.einsum("knw,knv->kwv", masked_local, solved, precision=lax.Precision.HIGHEST)
    shares = lax.psum_scatter(terms, "row", scatter_dimension=1, tiled=True)
    diag_block = diag_inverse - lax.psum(shares, "col")
    return (solved, diag_block)


def solution(mesh):
    placed = (P("row", "col"), P(None, ("row", "col"), None), P(None, "row", None), P(), P())
    return jax.shard_map(
        per_device,
        mesh=mesh,
        in_specs=placed,
        out_specs=(P(None, ("row", "col"), None), P(None, "row", None)),
        check_vma=False,
    )
```

profile of v0, /device:TPU:6, one launch (start us, length us, event | category | flops | bytes accessed | tf_op | source)
XLA Modules:
  0.0 864.0 jit_solution(14889107816256516591)
XLA Ops:
  7.2 0.0 copy-start
  7.2 0.0 all-gather.6.cloned.1.call-start
  7.2 1.7 fusion.21
  8.9 0.0 all-gather.6.cloned.1.call-update
  8.9 0.0 all-gather.4.cloned.1.call-start
  9.0 0.7 all-gather.4.cloned.1.call-update
  9.7 0.0 all-gather.8.cloned.1.call-start
  9.7 0.7 all-gather.8.cloned.1.call-update
  10.4 0.0 all-reduce.13.cloned.1.call-start
  10.5 0.7 iota_compare_fusion.5
  11.2 0.8 fusion.15
  12.0 0.4 fusion.3
  12.4 0.1 slice_reduce_fusion.2
  12.5 0.1 dynamic-slice.7
  12.5 0.1 dynamic-slice.6
  12.6 0.1 dynamic-slice.8
  12.7 64.1 %all-gather.6.cloned.1.call-done = f32[1,1536,256]{2,1,0:T(8,128)} async-done(((f32[1,48,256]{2,1,0:T(8,128)}), f32[1,1536,256]{2,1,0:T(8,128)}) %all-gather.6.cloned.1.call-update) | async-done | bytes 1572880 | tf_op jit(solution)/shard_map/all_gather | solution.py:56
  76.8 1.9 fusion.7
  78.7 64.3 %all-gather.4.cloned.1.call-done = f32[1,1536,256]{2,1,0:T(8,128)} async-done(((f32[1,48,256]{2,1,0:T(8,128)}), f32[1,1536,256]{2,1,0:T(8,128)}) %all-gather.4.cloned.1.call-update) | async-done | bytes 1572880 | tf_op jit(solution)/shard_map/all_gather | solution.py:56
  143.0 1.9 fusion.9
  144.9 63.8 %all-gather.8.cloned.1.call-done = f32[1,1536,256]{2,1,0:T(8,128)} async-done(((f32[1,48,256]{2,1,0:T(8,128)}), f32[1,1536,256]{2,1,0:T(8,128)}) %all-gather.8.cloned.1.call-update) | async-done | bytes 1572880 | tf_op jit(solution)/shard_map/all_gather | solution.py:56
  208.7 1.9 fusion.5
  210.5 0.0 all-reduce.13.cloned.1.call-update
  210.6 0.0 all-reduce.11.cloned.1.call-start
  210.6 95.0 %all-reduce.13.cloned.1.call-done = (f32[384,256]{1,0:T(8,128)}, f32[384,256]{1,0:T(8,128)}, f32[384,256]{1,0:T(8,128)}) async-done(((f32[384,256]{1,0:T(8,128)}, f32[384,256]{1,0:T(8,128)}, f32[384,256]{1,0:T(8,128)}), (f32[384,256]{1,0:T(8,128)}, f32[384,256]{1,0:T(8,128)}, f32[384,256]{1,0:T(8,128)})) %all-reduce.13.cloned.1.call-update) | async-done | bytes 1179664 | tf_op jit(solution)/shard_map/psum | solution.py:13
  305.6 0.0 copy-done
  305.6 6.2 fusion
  311.7 0.0 copy-start.4
  311.7 4.9 copy.21
  316.6 0.0 copy-done.4
  316.6 5.2 fusion.1
  321.8 0.0 copy-start.3
  321.8 4.9 copy.23
  326.6 0.0 copy-done.3
  326.6 5.2 fusion.2
  331.8 4.8 copy.25
  336.7 0.0 copy-start.6
  336.7 0.0 copy-start.1
  336.7 0.0 all-reduce.11.cloned.1.call-update
  336.7 0.0 copy-start.5
  336.7 0.0 reduce-scatter.2.cloned.1.call-start
  336.8 0.6 copy-done.6
  337.3 0.6 dynamic-slice
  338.6 0.2 fusion.16
  338.8 235.7 %all-reduce.11.cloned.1.call-done = (f32[1,1536,256]{2,0,1:T(1,128)}, f32[1,1536,256]{2,0,1:T(1,128)}, f32[1,1536,256]{2,0,1:T(1,128)}) async-done(((f32[1,1536,256]{2,0,1:T(1,128)}, f32[1,1536,256]{2,0,1:T(1,128)}, f32[1,1536,256]{2,0,1:T(1,128)}), (f32[1,1536,256]{2,0,1:T(1,128)}, f32[1,1536,256]{2,0,1:T(1,128)}, f32[1,1536,256]{2,0,1:T(1,128)})) %all-reduce.11.cloned.1.call-update) | async-done | bytes 4718608
  574.4 0.8 constant_dynamic-slice_fusion
  575.3 0.8 constant_dynamic-slice_fusion.2
  576.1 0.0 copy-done.1
  576.1 0.0 copy-start.2
  576.1 1.8 fusion.11
  578.0 0.0 reduce-scatter.2.cloned.1.call-update
  578.0 0.0 all-reduce.9.cloned.1.call-start
  578.1 76.2 %reduce-scatter.2.cloned.1.call-done = f32[3,32,256]{2,1,0:T(8,128)} async-done(((f32[3,256,256]{2,1,0:T(8,128)}), f32[3,32,256]{2,1,0:T(8,128)}) %reduce-scatter.2.cloned.1.call-update) | async-done | bytes 98320 | tf_op jit(solution)/shard_map/reduce_scatter | solution.py:69
  654.2 0.0 all-reduce.9.cloned.1.call-update
  654.3 201.3 %all-reduce.9.cloned.1.call-done = f32[3,32,256]{2,1,0:T(8,128)} async-done(((f32[3,32,256]{2,1,0:T(8,128)}), f32[3,32,256]{2,1,0:T(8,128)}) %all-reduce.9.cloned.1.call-update) | async-done | bytes 98320 | tf_op jit(solution)/shard_map/psum | solution.py:70
  855.6 0.0 copy-done.5
  855.6 1.5 sub.22
  857.1 0.0 copy-done.2
  (6 shorter events, 0.1 us)
Async XLA Ops:
  7.2 298.4 %copy-start = (f32[1536,384]{1,0:T(8,128)S(1)}, f32[1536,384]{1,0:T(8,128)}, u32[]{:S(2)}) copy-start(f32[1536,384]{1,0:T(8,128)} %param.5) | copy-start | bytes 7077892
  7.2 69.6 %all-gather.6.cloned.1.call-start = ((), (), s32[]{:S(2)}) async-start(), calls=%async_computation.2 | async-start | bytes 1622016 | tf_op jit(solution)/shard_map/all_gather | solution.py:56
  8.9 134.1 %all-gather.4.cloned.1.call-start = ((), (), s32[]{:S(2)}) async-start(), calls=%async_computation.1 | async-start | bytes 1622016 | tf_op jit(solution)/shard_map/all_gather | solution.py:56
  9.7 199.0 %all-gather.8.cloned.1.call-start = ((), (), s32[]{:S(2)}) async-start(), calls=%async_computation.3 | async-start | bytes 1622016 | tf_op jit(solution)/shard_map/all_gather | solution.py:56
  10.4 295.2 %all-reduce.13.cloned.1.call-start = ((), (), s32[]{:S(2)}) async-start(), calls=%async_computation.7 | async-start | bytes 2359296 | tf_op jit(solution)/shard_map/psum | solution.py:13
  210.6 363.9 %all-reduce.11.cloned.1.call-start = ((), (), s32[]{:S(2)}) async-start(), calls=%async_computation.6 | async-start | bytes 9437184
  311.7 4.9 copy-start.4
  321.8 4.9 copy-start.3
  336.7 0.7 copy-start.6
  336.7 239.5 %copy-start.1 = (f32[3,48,256]{2,1,0:T(8,128)S(1)}, f32[3,48,256]{2,1,0:T(8,128)}, u32[]{:S(2)}) copy-start(f32[3,48,256]{2,1,0:T(8,128)} %param.6) | copy-start | bytes 442372
  336.7 518.9 %copy-start.5 = (f32[3,32,256]{2,1,0:T(8,128)S(1)}, f32[3,32,256]{2,1,0:T(8,128)}, u32[]{:S(2)}) copy-start(f32[3,32,256]{2,1,0:T(8,128)} %param.7) | copy-start | bytes 294916
  336.7 317.5 %reduce-scatter.2.cloned.1.call-start = ((), (), s32[]{:S(2)}) async-start(), calls=%async_computation.4 | async-start | bytes 884736 | tf_op jit(solution)/shard_map/reduce_scatter | solution.py:69
  576.1 281.0 %copy-start.2 = (f32[3,48,256]{2,1,0:T(8,128)}, f32[3,48,256]{2,1,0:T(8,128)S(1)}, u32[]{:S(2)}) copy-start(f32[3,48,256]{2,1,0:T(8,128)S(1)} %pad_maximum_fusion) | copy-start | bytes 442372
  578.0 277.5 %all-reduce.9.cloned.1.call-start = ((), (), s32[]{:S(2)}) async-start(), calls=%async_computation.5 | async-start | bytes 196608 | tf_op jit(solution)/shard_map/psum | solution.py:70
Sparse Core Ops, SparseCore 0:
  10.4 66.3 all-gather.5
  79.2 63.7 all-gather.3
  144.9 63.7 all-gather.7
  211.4 94.1 all-reduce.12
  336.8 237.5 all-reduce.10
  578.1 76.0 reduce-scatter.1
  656.9 198.6 all-reduce.8
where the time goes:
time: 865 us; the launch traced here: 864 us
  waiting for transfers between devices  802 us (93%)
  local copies, waits for them, and re-layouts  19.3 us (2%)
  matrix products  18.9 us (2%)
  between operations  14.9 us (2%)
  other arithmetic  8.73 us (1%)
    unnamed x8, waiting for transfers between devices  237 us
    psum x1, waiting for transfers between devices, per_device(): diag_block = diag_inverse - lax.psum(shares, 'col')  201 us
    all_gather x3, waiting for transfers between devices, per_device(): lax.all_gather(factor_panel[member:member + 1], 'col', axis=1, tiled=True)  192 us
    psum x1, waiting for transfers between devices, broadcast(): return lax.psum(block, axis)  95 us
    reduce_scatter x1, waiting for transfers between devices, per_device(): shares = lax.psum_scatter(terms, 'row', scatter_dimension=1, tiled=True)  76.2 us
  transfers between devices with their start and end apart: 7, of which 7 were waited for; matrix products, arithmetic and copies ran while one was open for 1% of the time, Pallas kernels for 0%

commit v1 on v0

--- a/solution.py
+++ b/solution.py
@@ -53,7 +53,12 @@
     start_col = col_id % group_ratio * span_col
     solved_parts = []
     for member in range(NSN):
-        gathered = lax.all_gather(factor_panel[member : member + 1], "col", axis=1, tiled=True)
+        gathered = jnp.concatenate(
+            lax.all_to_all(
+                jnp.stack([factor_panel[member : member + 1]] * lax.axis_size("col")), "col", 0, 0
+            ),
+            axis=1,
+        )
         masked_range = gathered * mask_range[member : member + 1, :, None]
         piece = lax.dynamic_slice_in_dim(masked_range, start_col, span_col, 1)
         columns = broadcast(piece, "row", source_row)

time: 865 us -> 803 us (0.928)
  waiting for transfers between devices: 802 us -> 640 us
  blocking collectives: 0 us -> 94.4 us
    all_gather x3 -> x0, waiting for transfers between devices: 192 us -> none  [per_device(): lax.all_gather(factor_panel[member:member + 1], 'col', axis=1, tiled=True)]
    all_to_all x0 -> x2, blocking collectives: none -> 94.4 us  [per_device(): lax.all_to_all(jnp.stack([factor_panel[member:member + 1]] * lax.axis_siz...]
    all_to_all x0 -> x1, waiting for transfers between devices: none -> 33.1 us  [per_device(): lax.all_to_all(jnp.stack([factor_panel[member:member + 1]] * lax.axis_siz...]
    unnamed x8 -> x5, waiting for transfers between devices: 237 us -> 236 us
  transfers between devices with their start and end apart: 7 -> 5, of which waited for: 7 -> 5; matrix products, arithmetic and copies ran while one was open for 1% -> 1% of each run, Pallas kernels for 0% -> 0%
where the time goes in v1:
time: 803 us; the launch traced here: 802 us
  waiting for transfers between devices  640 us (80%)
  blocking collectives  94.4 us (12%)
  local copies, waits for them, and re-layouts  20.4 us (3%)
  matrix products  18.9 us (2%)
  between operations  14.6 us (2%)
    unnamed x5, waiting for transfers between devices  236 us
    psum x1, waiting for transfers between devices, per_device(): diag_block = diag_inverse - lax.psum(shares, 'col')  201 us
    all_to_all x2, blocking collectives, per_device(): lax.all_to_all(jnp.stack([factor_panel[member:member + 1]] * lax.axis_siz...  94.4 us
    psum x1, waiting for transfers between devices, broadcast(): return lax.psum(block, axis)  93.4 us
    reduce_scatter x1, waiting for transfers between devices, per_device(): shares = lax.psum_scatter(terms, 'row', scatter_dimension=1, tiled=True)  76.3 us
    all_to_all x1, waiting for transfers between devices, per_device(): lax.all_to_all(jnp.stack([factor_panel[member:member + 1]] * lax.axis_siz...  33.1 us
    dot_general x3, matrix products, apply_block(): summed = jnp.dot(inverse_block, panel_rows, precision=lax.Precision.HIGHEST)  16.5 us
  transfers between devices with their start and end apart: 5, of which 5 were waited for; matrix products, arithmetic and copies ran while one was open for 1% of the time, Pallas kernels for 0%

profile of v1, /device:TPU:6, one launch (start us, length us, event | category | flops | bytes accessed | tf_op | source)
XLA Modules:
  0.0 801.7 jit_solution(12433806089949368829)
XLA Ops:
  7.2 0.0 copy-start
  7.2 1.0 slice_bitcast_fusion.2
  8.2 0.2 stack.7
  8.4 49.8 %all_to_all.15 = f32[32,1,48,256]{3,2,1,0:T(8,128)} all-to-all(f32[32,1,48,256]{3,2,1,0:T(8,128)S(1)} %stack.7), channel_id=1, replica_groups=mesh['row'=8,'col'=32] {'col'}, dimensions={0} | all-to-all | bytes 3145728 | tf_op jit(solution)/shard_map/all_to_all | solution.py:57
  58.1 0.2 stack.6
  58.3 44.6 %all_to_all.16 = f32[32,1,48,256]{3,2,1,0:T(8,128)} all-to-all(f32[32,1,48,256]{3,2,1,0:T(8,128)S(1)} %stack.6), channel_id=1, replica_groups=mesh['row'=8,'col'=32] {'col'}, dimensions={0} | all-to-all | bytes 3145728 | tf_op jit(solution)/shard_map/all_to_all | solution.py:57
  102.9 1.3 stack.8
  104.3 0.0 copy-start.7
  104.3 0.0 copy-start.6
  104.3 6.1 all-to-all-start.2
  110.4 0.0 all-reduce.13.cloned.1.call-start
  110.5 0.0 copy-done.7
  110.5 0.1 iota_compare_fusion.5
  110.6 0.0 copy-done.6
  110.6 0.1 fusion.15
  110.7 0.4 fusion.3
  111.1 0.1 slice_reduce_fusion.2
  111.2 0.1 dynamic-slice.7
  111.2 0.1 dynamic-slice.6
  111.3 0.1 dynamic-slice.8
  111.4 1.9 fusion.7
  113.3 1.9 fusion.9
  115.1 33.1 %all-to-all-done.2 = f32[32,1,48,256]{3,2,1,0:T(8,128)} async-done(((f32[32,1,48,256]{3,2,1,0:T(8,128)}), f32[32,1,48,256]{3,2,1,0:T(8,128)}, u32[]{:S(2)}, u32[]{:S(2)}) %all-to-all-start.2) | async-done | bytes 1572896 | tf_op jit(solution)/shard_map/all_to_all | solution.py:57
  148.3 1.9 fusion.5
  150.1 0.0 all-reduce.13.cloned.1.call-update
  150.2 0.0 all-reduce.11.cloned.1.call-start
  150.2 93.4 %all-reduce.13.cloned.1.call-done = (f32[384,256]{1,0:T(8,128)}, f32[384,256]{1,0:T(8,128)}, f32[384,256]{1,0:T(8,128)}) async-done(((f32[384,256]{1,0:T(8,128)}, f32[384,256]{1,0:T(8,128)}, f32[384,256]{1,0:T(8,128)}), (f32[384,256]{1,0:T(8,128)}, f32[384,256]{1,0:T(8,128)}, f32[384,256]{1,0:T(8,128)})) %all-reduce.13.cloned.1.call-update) | async-done | bytes 1179664 | tf_op jit(solution)/shard_map/psum | solution.py:13
  243.6 0.0 copy-done
  243.6 6.2 fusion
  249.8 0.0 copy-start.4
  249.8 4.9 copy.21
  254.6 0.0 copy-done.4
  254.6 5.2 fusion.1
  259.8 0.0 copy-start.3
  259.8 4.9 copy.23
  264.7 0.0 copy-done.3
  264.7 5.2 fusion.2
  269.9 4.8 copy.25
  274.7 0.0 copy-start.8
  274.7 0.0 copy-start.1
  274.7 0.0 all-reduce.11.cloned.1.call-update
  274.7 0.0 copy-start.5
  274.8 0.0 reduce-scatter.2.cloned.1.call-start
  274.8 0.6 copy-done.8
  275.4 0.6 dynamic-slice
  276.6 0.2 fusion.16
  276.8 235.7 %all-reduce.11.cloned.1.call-done = (f32[1,1536,256]{2,0,1:T(1,128)}, f32[1,1536,256]{2,0,1:T(1,128)}, f32[1,1536,256]{2,0,1:T(1,128)}) async-done(((f32[1,1536,256]{2,0,1:T(1,128)}, f32[1,1536,256]{2,0,1:T(1,128)}, f32[1,1536,256]{2,0,1:T(1,128)}), (f32[1,1536,256]{2,0,1:T(1,128)}, f32[1,1536,256]{2,0,1:T(1,128)}, f32[1,1536,256]{2,0,1:T(1,128)})) %all-reduce.11.cloned.1.call-update) | async-done | bytes 4718608
  512.5 0.8 constant_dynamic-slice_fusion
  513.4 0.8 constant_dynamic-slice_fusion.2
  514.2 0.0 copy-done.1
  514.2 0.0 copy-start.2
  514.2 1.8 fusion.11
  516.1 0.0 reduce-scatter.2.cloned.1.call-update
  516.1 0.0 all-reduce.9.cloned.1.call-start
  516.2 76.3 %reduce-scatter.2.cloned.1.call-done = f32[3,32,256]{2,1,0:T(8,128)} async-done(((f32[3,256,256]{2,1,0:T(8,128)}), f32[3,32,256]{2,1,0:T(8,128)}) %reduce-scatter.2.cloned.1.call-update) | async-done | bytes 98320 | tf_op jit(solution)/shard_map/reduce_scatter | solution.py:74
  592.5 0.0 all-reduce.9.cloned.1.call-update
  592.5 201.1 %all-reduce.9.cloned.1.call-done = f32[3,32,256]{2,1,0:T(8,128)} async-done(((f32[3,32,256]{2,1,0:T(8,128)}), f32[3,32,256]{2,1,0:T(8,128)}) %all-reduce.9.cloned.1.call-update) | async-done | bytes 98320 | tf_op jit(solution)/shard_map/psum | solution.py:75
  793.6 0.0 copy-done.5
  793.6 1.5 sub.22
  795.2 0.0 copy-done.2
  (6 shorter events, 0.1 us)
Async XLA Ops:
  7.2 236.4 %copy-start = (f32[1536,384]{1,0:T(8,128)S(1)}, f32[1536,384]{1,0:T(8,128)}, u32[]{:S(2)}) copy-start(f32[1536,384]{1,0:T(8,128)} %param.5) | copy-start | bytes 7077892
  104.3 6.2 copy-start.7
  104.3 6.3 copy-start.6
  104.3 44.0 %all-to-all-start.2 = ((f32[32,1,48,256]{3,2,1,0:T(8,128)}), f32[32,1,48,256]{3,2,1,0:T(8,128)}, u32[]{:S(2)}, u32[]{:S(2)}) async-start(f32[32,1,48,256]{3,2,1,0:T(8,128)} %stack.8), calls=%async_computation.2 | async-start | bytes 3145728 | tf_op jit(solution)/shard_map/all_to_all | solution.py:57
  110.4 133.2 %all-reduce.13.cloned.1.call-start = ((), (), s32[]{:S(2)}) async-start(), calls=%async_computation.7 | async-start | bytes 2359296 | tf_op jit(solution)/shard_map/psum | solution.py:13
  150.2 362.4 %all-reduce.11.cloned.1.call-start = ((), (), s32[]{:S(2)}) async-start(), calls=%async_computation.6 | async-start | bytes 9437184
  249.8 4.9 copy-start.4
  259.8 4.9 copy-start.3
  274.7 0.7 copy-start.8
  274.7 239.5 %copy-start.1 = (f32[3,48,256]{2,1,0:T(8,128)S(1)}, f32[3,48,256]{2,1,0:T(8,128)}, u32[]{:S(2)}) copy-start(f32[3,48,256]{2,1,0:T(8,128)} %param.6) | copy-start | bytes 442372
  274.7 518.9 %copy-start.5 = (f32[3,32,256]{2,1,0:T(8,128)S(1)}, f32[3,32,256]{2,1,0:T(8,128)}, u32[]{:S(2)}) copy-start(f32[3,32,256]{2,1,0:T(8,128)} %param.7) | copy-start | bytes 294916
  274.8 317.7 %reduce-scatter.2.cloned.1.call-start = ((), (), s32[]{:S(2)}) async-start(), calls=%async_computation.4 | async-start | bytes 884736 | tf_op jit(solution)/shard_map/reduce_scatter | solution.py:74
  514.2 281.0 %copy-start.2 = (f32[3,48,256]{2,1,0:T(8,128)}, f32[3,48,256]{2,1,0:T(8,128)S(1)}, u32[]{:S(2)}) copy-start(f32[3,48,256]{2,1,0:T(8,128)S(1)} %pad_maximum_fusion) | copy-start | bytes 442372
  516.1 277.5 %all-reduce.9.cloned.1.call-start = ((), (), s32[]{:S(2)}) async-start(), calls=%async_computation.5 | async-start | bytes 196608 | tf_op jit(solution)/shard_map/psum | solution.py:75
Sparse Core Ops, SparseCore 0:
  150.3 93.2 all-reduce.12
  274.9 237.6 all-reduce.10
  516.4 76.0 reduce-scatter.1
  595.0 198.6 all-reduce.8
